TPU v7x, 32 devices: a whole 2x2x4 slice. The times are simulated.
32 devices in a mesh: seq: 2 (over y), dp: 16 (over z, x, core).
Axes of the slice: x: 2, y: 2, z: 4, core: 2. Of those that a mesh axis runs over, the one named last changes fastest.
Arguments:
- tokens: bfloat16 [16, 512, 1024], P('dp', 'seq'), may hold values from -6 to 6
- starts: int32 [16, 512], P('dp', 'seq'), may hold values 0 or 1
- routes: int32 [16, 512, 8], P('dp', 'seq'), may hold values from 0 to 15, all different within a row; in each aligned block of 256 rows (0 to 255, 256 to 511, ..., all dimensions but the last counted through in order) at most 224 rows name the same one
- gain_one: bfloat16 [1024], P('dp'), may hold values from 0.5 to 1.5
- query_key_value_weight: bfloat16 [1024, 2048], P('dp'), may hold values from -0.1875 to 0.1875
- w_out: bfloat16 [1024, 1024], P('dp'), may hold values from -1.5 to 1.5
- gain_two: bfloat16 [1024], P('dp'), may hold values from 0.5 to 1.5
- w_router: bfloat16 [1024, 16], P('dp'), may hold values from -0.09375 to 0.09375
- w_gate_up: bfloat16 [1024, 16, 1024], P('dp'), may hold values from -0.1875 to 0.1875
- w_down: bfloat16 [512, 16, 1024], P('dp'), may hold values from -1 to 1
- cotangent: bfloat16 [16, 512, 1024], P('dp', 'seq'), may hold values from -6 to 6
Outputs:
- output: bfloat16 [16, 512, 1024], P('dp', 'seq')
- input_grad: bfloat16 [16, 512, 1024], P('dp', 'seq')
- grad_gain_one: float32 [1024], P('dp')
- grad_w_qkv: float32 [1024, 2048], P('dp')
- grad_w_out: float32 [1024, 1024], P('dp')
- grad_gain_two: float32 [1024], P('dp')
- grad_w_router: float32 [1024, 16], P('dp')
- grad_w_gate_up: float32 [1024, 16, 1024], P('dp')
- grad_w_down: float32 [512, 16, 1024], P('dp')
- stream_rms: float32 [16, 2], P('dp')
Inputs may be any that keep to these rules, and one draw needn't show every extreme that they name: `starts`: 1 marks a token that begins a document; a stream's first token begins one whatever its entry. `routes`: each row names 8 different experts; within the 256 rows of one device no expert is named more than 224 times, and in every draw some expert is named exactly 224 times on some device.
All inputs are finite; a program needn't handle non-finite values. No bound on the sum of `starts` on one device may be relied on, other than what follows from the above.
Results may differ from a plain program's by a relative error of at most 0.015.
Values may be sent and summed in bfloat16 or wider, within the bound.
A program may use at most 384 MiB of HBM per device.

v0:
```python
import jax
import jax.numpy as jnp
from jax import lax
from jax.sharding import PartitionSpec as P

MODEL_WIDTH = 1024
QUERY_HEADS = 16
KEY_VALUE_HEADS = 8
HEAD_SIZE = 64
F = 512
EXPERTS = 16
TOPK = 8
CAP = 224
epsilon = 1e-06
rope_base = 10000.0
highest = lax.Precision.HIGHEST
masked_score = -1e30


def rms_normed(token_rows, gain_row):
    inverse = lax.rsqrt(jnp.mean(token_rows * token_rows, axis=-1, keepdims=True) + epsilon)
    return token_rows * inverse * gain_row


def norm_back(token_rows, gain_row, upstream):
    inverse = lax.rsqrt(jnp.mean(token_rows * token_rows, axis=-1, keepdims=True) + epsilon)
    gain_grad = jnp.sum(upstream * token_rows * inverse, axis=0)
    scaled = upstream * gain_row
    rows_grad = inverse * scaled - token_rows * inverse**3 * jnp.mean(
        scaled * token_rows, axis=-1, keepdims=True
    )
    return (rows_grad, gain_grad)


def rope_tables(positions, head_dim):
    half_dim = head_dim // 2
    frequency = rope_base ** (-(jnp.arange(half_dim, dtype=jnp.float32) * 2.0) / head_dim)
    angles = positions.astype(jnp.float32)[:, None] * frequency[None, :]
    cosine_table = jnp.cos(angles)
    sine_values = jnp.sin(angles)
    return (
        jnp.concatenate([cosine_table, cosine_table], 1),
        jnp.concatenate([sine_values, sine_values], 1),
    )


def rotary_apply(head_rows, cosine_table, sine_values):
    half_dim = head_rows.shape[-1] // 2
    turned = jnp.concatenate([-head_rows[..., half_dim:], head_rows[..., :half_dim]], -1)
    return head_rows * cosine_table[:, None, :] + turned * sine_values[:, None, :]


def unrotate(grad_rows, cosine_table, sine_values):
    half_dim = grad_rows.shape[-1] // 2
    scaled = grad_rows * sine_values[:, None, :]
    back_turn = jnp.concatenate([scaled[..., half_dim:], -scaled[..., :half_dim]], -1)
    return grad_rows * cosine_table[:, None, :] + back_turn


def slot_tables(route_rows):
    pair_count = route_rows.shape[0] * route_rows.shape[1]
    flat_routes = route_rows.reshape(-1)
    one_hot = (flat_routes[:, None] == jnp.arange(EXPERTS, dtype=jnp.int32)[None, :]).astype(
        jnp.int32
    )
    earlier = jnp.cumsum(one_hot, axis=0) - one_hot
    within = jnp.sum(earlier * one_hot, axis=1)
    slot_flat = flat_routes * CAP + within
    pair_of_slot = (
        jnp.full((EXPERTS * CAP,), pair_count, jnp.int32)
        .at[slot_flat]
        .set(jnp.arange(pair_count, dtype=jnp.int32))
    )
    return (slot_flat.reshape(route_rows.shape), pair_of_slot)


def swiglu_parts(gate_up):
    gate_part = gate_up[..., :F]
    up_part = gate_up[..., F:]
    sigmoid_gate = jax.nn.sigmoid(gate_part)
    silu_gate = gate_part * sigmoid_gate
    act_low = (silu_gate * up_part).astype(jnp.bfloat16)
    return (gate_part, up_part, sigmoid_gate, silu_gate, act_low)


def swiglu_back(act_grad, gate_part, up_part, sigmoid_gate, silu_gate):
    gate_deriv = sigmoid_gate * (1.0 + gate_part * (1.0 - sigmoid_gate))
    return jnp.concatenate([act_grad * up_part * gate_deriv, act_grad * silu_gate], -1).astype(
        jnp.bfloat16
    )


def body(
    tokens,
    starts,
    routes,
    gain_one,
    query_key_value_weight,
    w_out,
    gain_two,
    w_router,
    w_gate_up,
    w_down,
    cotangent,
):
    token_count = tokens.shape[1]
    seq_rank = lax.axis_index("seq")
    token_rows = tokens[0].astype(jnp.float32)
    grad_output = cotangent[0].astype(jnp.float32)
    stream_flags = lax.all_gather(starts[0], "seq", axis=0, tiled=True)
    stream_index = jnp.arange(stream_flags.shape[0], dtype=jnp.int32)
    begins = jnp.where(stream_index == 0, 1, stream_flags)
    segment_all = jnp.cumsum(begins)
    last_begin = lax.cummax(jnp.where(begins > 0, stream_index, -1), axis=0)
    positions_all = stream_index - last_begin
    positions = lax.dynamic_slice_in_dim(positions_all, seq_rank * token_count, token_count)
    gain_one_all, qkv_weight, out_weight, gain_two_all, router_weight = (
        lax.all_gather(gain_one, "dp", axis=0, tiled=True),
        lax.all_gather(query_key_value_weight, "dp", axis=0, tiled=True),
        lax.all_gather(w_out, "dp", axis=0, tiled=True),
        lax.all_gather(gain_two, "dp", axis=0, tiled=True),
        lax.all_gather(w_router, "dp", axis=0, tiled=True),
    )
    gain_a = gain_one_all.astype(jnp.float32)
    gain_b = gain_two_all.astype(jnp.float32)
    query_columns = QUERY_HEADS * HEAD_SIZE
    key_value_columns = KEY_VALUE_HEADS * HEAD_SIZE
    normed_one = rms_normed(token_rows, gain_a).astype(jnp.bfloat16)
    projected_rows = jnp.dot(normed_one, qkv_weight, preferred_element_type=jnp.float32)
    cosine_table, sine_values = rope_tables(positions, HEAD_SIZE)
    queries_low = (
        rotary_apply(
            projected_rows[:, :query_columns].reshape(token_count, QUERY_HEADS, HEAD_SIZE),
            cosine_table,
            sine_values,
        )
        .reshape(token_count, query_columns)
        .astype(jnp.bfloat16)
    )
    keys_low = (
        rotary_apply(
            projected_rows[:, query_columns : query_columns + key_value_columns].reshape(
                token_count, KEY_VALUE_HEADS, HEAD_SIZE
            ),
            cosine_table,
            sine_values,
        )
        .reshape(token_count, key_value_columns)
        .astype(jnp.bfloat16)
    )
    values_low = projected_rows[:, query_columns + key_value_columns :].astype(jnp.bfloat16)
    query_heads, key_heads, value_heads = (
        lax.all_to_all(queries_low, "seq", split_axis=1, concat_axis=0, tiled=True),
        lax.all_to_all(keys_low, "seq", split_axis=1, concat_axis=0, tiled=True),
        lax.all_to_all(values_low, "seq", split_axis=1, concat_axis=0, tiled=True),
    )
    sequence_length = query_heads.shape[0]
    kv_local = key_heads.shape[1] // HEAD_SIZE
    query_group_width = QUERY_HEADS // KEY_VALUE_HEADS
    query_four = query_heads.reshape(sequence_length, kv_local, query_group_width, HEAD_SIZE)
    key_three = key_heads.reshape(sequence_length, kv_local, HEAD_SIZE)
    value_three = value_heads.reshape(sequence_length, kv_local, HEAD_SIZE)
    block_rows = min(512, sequence_length)
    score_scale = HEAD_SIZE ** (-0.5)
    key_index = jnp.arange(sequence_length, dtype=jnp.int32)

    def block_scores(row_start):
        scores = (
            jnp.einsum("qgrd,kgd->grqk", query_four, key_three, preferred_element_type=jnp.float32)
            * score_scale
        )
        query_index = row_start + jnp.arange(block_rows, dtype=jnp.int32)
        allowed = (segment_all[:, None] == segment_all[None, :]) & (
            key_index[None, :] <= query_index[:, None]
        )
        return (query_four, jnp.where(allowed[None, None], scores, masked_score))

    row_start = 0
    query_block, scores = block_scores(row_start)
    top_score = jnp.max(scores, axis=-1, keepdims=True)
    exp_scores = jnp.exp(scores - top_score)
    exp_total = jnp.sum(exp_scores, axis=-1, keepdims=True)
    probs_low = (exp_scores / exp_total).astype(jnp.bfloat16)
    block_out = jnp.einsum(
        "grqk,kgd->qgrd", probs_low, value_three, preferred_element_type=jnp.float32
    )
    outputs_list = block_out.reshape(block_rows, kv_local * query_group_width * HEAD_SIZE).astype(
        jnp.bfloat16
    )
    log_sums = [top_score + jnp.log(exp_total)]
    attended = lax.all_to_all(outputs_list, "seq", split_axis=0, concat_axis=1, tiled=True)
    hidden = token_rows + jnp.dot(attended, out_weight, preferred_element_type=jnp.float32)
    normed_two = rms_normed(hidden, gain_b).astype(jnp.bfloat16)
    logits = jnp.dot(normed_two, router_weight, preferred_element_type=jnp.float32)
    route_rows = routes[0]
    route_match = route_rows[:, :, None] == jnp.arange(EXPERTS, dtype=jnp.int32)[None, None, :]
    chosen = jnp.sum(jnp.where(route_match, logits[:, None, :], 0.0), axis=-1)
    gate_weights = jax.nn.softmax(chosen, axis=-1)
    slot_index, pair_of_slot = slot_tables(route_rows)
    token_of_slot = pair_of_slot // TOPK
    padded = jnp.concatenate([normed_two, jnp.zeros((1, MODEL_WIDTH), jnp.bfloat16)], 0)
    dispatched = padded[token_of_slot].reshape(EXPERTS, CAP, MODEL_WIDTH)
    pair_gate = jnp.concatenate([gate_weights.reshape(-1), jnp.zeros((1,), jnp.float32)])[
        pair_of_slot
    ]
    grad_padded = jnp.concatenate([grad_output, jnp.zeros((1, MODEL_WIDTH), jnp.float32)], 0)
    expert_grad = (
        (pair_gate[:, None] * grad_padded[token_of_slot])
        .astype(jnp.bfloat16)
        .reshape(EXPERTS, CAP, MODEL_WIDTH)
    )
    full_gate_up, full_down = (
        lax.all_gather(w_gate_up, "dp", axis=0, tiled=True),
        lax.all_gather(w_down, "dp", axis=0, tiled=True),
    )
    gate_up = jnp.einsum(
        "ecd,def->ecf", dispatched, full_gate_up, preferred_element_type=jnp.float32
    )
    gate_part, up_part, sigmoid_gate, silu_gate, act_low = swiglu_parts(gate_up)
    expert_out = jnp.einsum("ecf,fed->ecd", act_low, full_down, preferred_element_type=jnp.float32)
    act_grad = jnp.einsum(
        "ecd,fed->ecf", expert_grad, full_down, preferred_element_type=jnp.float32
    )
    down_wgrad = jnp.einsum(
        "ecf,ecd->fed", act_low, expert_grad, preferred_element_type=jnp.float32
    )
    gate_up_grad = swiglu_back(act_grad, gate_part, up_part, sigmoid_gate, silu_gate)
    gate_up_wgrad = jnp.einsum(
        "ecd,ecf->def", dispatched, gate_up_grad, preferred_element_type=jnp.float32
    )
    dispatched_grad = jnp.einsum(
        "ecf,def->ecd", gate_up_grad, full_gate_up, preferred_element_type=jnp.float32
    )
    expert_flat = expert_out.reshape(EXPERTS * CAP, MODEL_WIDTH)
    picked = expert_flat[slot_index]
    mixed = jnp.sum(gate_weights[:, :, None] * picked, axis=1)
    output = (hidden + mixed).astype(jnp.bfloat16)[None]
    stat_sums = jnp.stack([jnp.sum(hidden * hidden), jnp.sum(mixed * mixed)])
    gate_grad = jnp.sum(picked * grad_output[:, None, :], axis=-1)
    normed_grad = jnp.sum(dispatched_grad.reshape(EXPERTS * CAP, MODEL_WIDTH)[slot_index], axis=1)
    chosen_grad = gate_weights * (
        gate_grad - jnp.sum(gate_weights * gate_grad, axis=-1, keepdims=True)
    )
    logits_grad = jnp.sum(jnp.where(route_match, chosen_grad[:, :, None], 0.0), axis=1)
    router_float = router_weight.astype(jnp.float32)
    normed_grad = normed_grad + jnp.dot(logits_grad, router_float.T, precision=highest)
    router_wgrad = jnp.dot(normed_two.astype(jnp.float32).T, logits_grad, precision=highest)
    hidden_branch, gain_two_grad = norm_back(hidden, gain_b, normed_grad)
    hidden_grad = grad_output + hidden_branch
    branch_low = hidden_grad.astype(jnp.bfloat16)
    out_wgrad = jnp.einsum("tc,td->cd", attended, branch_low, preferred_element_type=jnp.float32)
    attended_grad = jnp.einsum(
        "td,cd->tc", branch_low, out_weight, preferred_element_type=jnp.float32
    ).astype(jnp.bfloat16)
    attended_grad_heads = lax.all_to_all(
        attended_grad, "seq", split_axis=1, concat_axis=0, tiled=True
    )
    row_start = 0
    query_block, scores = block_scores(row_start)
    probs = jnp.exp(scores - log_sums[row_start // block_rows])
    grad_block = attended_grad_heads.reshape(block_rows, kv_local, query_group_width, HEAD_SIZE)
    prob_grad = jnp.einsum(
        "qgrd,kgd->grqk", grad_block, value_three, preferred_element_type=jnp.float32
    )
    row_delta = jnp.sum(probs * prob_grad, axis=-1, keepdims=True)
    score_grad = (probs * (prob_grad - row_delta)).astype(jnp.bfloat16)
    block_query_grad = (
        jnp.einsum("grqk,kgd->qgrd", score_grad, key_three, preferred_element_type=jnp.float32)
        * score_scale
    )
    query_grads = block_query_grad.reshape(block_rows, kv_local * query_group_width * HEAD_SIZE)
    key_grad = (
        jnp.einsum("grqk,qgrd->kgd", score_grad, query_block, preferred_element_type=jnp.float32)
        * score_scale
    )
    value_grad = jnp.einsum(
        "grqk,qgrd->kgd", probs.astype(jnp.bfloat16), grad_block, preferred_element_type=jnp.float32
    )
    query_grad_low = query_grads.astype(jnp.bfloat16)
    key_grad_low = key_grad.reshape(sequence_length, kv_local * HEAD_SIZE).astype(jnp.bfloat16)
    value_grad_low = value_grad.reshape(sequence_length, kv_local * HEAD_SIZE).astype(jnp.bfloat16)
    query_grad_tok, key_grad_token_rows, value_grad_tok = (
        lax.all_to_all(query_grad_low, "seq", split_axis=0, concat_axis=1, tiled=True),
        lax.all_to_all(key_grad_low, "seq", split_axis=0, concat_axis=1, tiled=True),
        lax.all_to_all(value_grad_low, "seq", split_axis=0, concat_axis=1, tiled=True),
    )
    query_back = unrotate(
        query_grad_tok.astype(jnp.float32).reshape(token_count, QUERY_HEADS, HEAD_SIZE),
        cosine_table,
        sine_values,
    ).reshape(token_count, query_columns)
    key_back = unrotate(
        key_grad_token_rows.astype(jnp.float32).reshape(token_count, KEY_VALUE_HEADS, HEAD_SIZE),
        cosine_table,
        sine_values,
    ).reshape(token_count, key_value_columns)
    projected_grad = jnp.concatenate(
        [query_back, key_back, value_grad_tok.astype(jnp.float32)], 1
    ).astype(jnp.bfloat16)
    qkv_wgrad = jnp.einsum(
        "td,tc->dc", normed_one, projected_grad, preferred_element_type=jnp.float32
    )
    normed_one_grad = jnp.einsum(
        "tc,dc->td", projected_grad, qkv_weight, preferred_element_type=jnp.float32
    )
    rows_branch, gain_one_grad = norm_back(token_rows, gain_a, normed_one_grad)
    input_grad = (hidden_grad + rows_branch).astype(jnp.bfloat16)[None]
    (
        shard_gain_one,
        shard_qkv,
        shard_out,
        shard_gain_two,
        shard_router,
        shard_gate_up,
        shard_down,
    ) = (
        lax.psum_scatter(gain_one_grad, "dp", scatter_dimension=0, tiled=True),
        lax.psum_scatter(qkv_wgrad, "dp", scatter_dimension=0, tiled=True),
        lax.psum_scatter(out_wgrad, "dp", scatter_dimension=0, tiled=True),
        lax.psum_scatter(gain_two_grad, "dp", scatter_dimension=0, tiled=True),
        lax.psum_scatter(router_wgrad, "dp", scatter_dimension=0, tiled=True),
        lax.psum_scatter(gate_up_wgrad, "dp", scatter_dimension=0, tiled=True),
        lax.psum_scatter(down_wgrad, "dp", scatter_dimension=0, tiled=True),
    )
    summed = (
        lax.psum(shard_gain_one.astype(jnp.bfloat16), "seq").astype(jnp.float32),
        lax.psum(shard_qkv.astype(jnp.bfloat16), "seq").astype(jnp.float32),
        lax.psum(shard_out.astype(jnp.bfloat16), "seq").astype(jnp.float32),
        lax.psum(shard_gain_two.astype(jnp.bfloat16), "seq").astype(jnp.float32),
        lax.psum(shard_router.astype(jnp.bfloat16), "seq").astype(jnp.float32),
        lax.psum(shard_gate_up.astype(jnp.bfloat16), "seq").astype(jnp.float32),
        lax.psum(shard_down.astype(jnp.bfloat16), "seq").astype(jnp.float32),
        lax.psum(stat_sums.astype(jnp.bfloat16), "seq").astype(jnp.float32),
    )
    stream_rms = jnp.sqrt(summed[7] / (sequence_length * MODEL_WIDTH)).reshape(1, 2)
    return (
        output,
        input_grad,
        summed[0],
        summed[1],
        summed[2],
        summed[3],
        summed[4],
        summed[5],
        summed[6],
        stream_rms,
    )


def solution(mesh):
    placed = (
        P("dp", "seq", None),
        P("dp", "seq"),
        P("dp", "seq", None),
        P("dp"),
        P("dp", None),
        P("dp", None),
        P("dp"),
        P("dp", None),
        P("dp", None, None),
        P("dp", None, None),
        P("dp", "seq", None),
    )
    return jax.shard_map(
        body,
        mesh=mesh,
        in_specs=placed,
        out_specs=(
            P("dp", "seq", None),
            P("dp", "seq", None),
            P("dp"),
            P("dp", None),
            P("dp", None),
            P("dp"),
            P("dp", None),
            P("dp", None, None),
            P("dp", None, None),
            P("dp", None),
        ),
        check_vma=False,
    )
```

profile of v0, /device:TPU:0, one launch (start us, length us, event | category | flops | bytes accessed | tf_op | source)
XLA Modules:
  0.0 1841.7 jit_solution(11289706347054955673)
XLA Ops:
  16.7 35.8 %all-reduce.7 = (bf16[1024]{0:T(1024)(128)(2,1)S(1)}, bf16[1024]{0:T(1024)(128)(2,1)S(1)}) all-reduce(bf16[1024]{0:T(1024)(128)(2,1)S(1)} %dynamic-update-slice, bf16[1024]{0:T(1024)(128)(2,1)S(1)} %dynamic-update-slice.1), channel_id=1, replica_groups=mesh['seq'=2,'dp'=16] {'dp'}, use_global_device_ids=true, to_apply=%add.2 | all-reduce | flops 2048 | bytes 8192
  65.4 8.1 scatter_custom_fusion
  132.6 18.3 all-gather.1
  151.3 12.5 gather_fusion.3
  168.6 18.9 %gather_fusion.2 = f32[3584]{0:T(1024)S(1)} fusion(f32[2049]{0:T(1024)S(1)} %pad_maximum_fusion.10, s32[4096]{0:T(1024)S(1)} %get-tuple-element.83), kind=kCustom, calls=%fused_computation.2 | custom fusion | bytes 43008 | tf_op jit(solution)/shard_map/gather | solution.py:203
  187.6 11.9 gather_fusion
  199.6 75.6 %all-gather.11.cloned.1.call-done = bf16[1024,16,1024]{2,0,1:T(8,128)(2,1)} async-done(((bf16[64,16,1024]{2,0,1:T(8,128)(2,1)}), bf16[1024,16,1024]{2,0,1:T(8,128)(2,1)}) %all-gather.11.cloned.1.call-update) | async-done | bytes 33554448 | tf_op jit(solution)/shard_map/all_gather | solution.py:213
  275.1 23.0 %fusion.81 = f32[16,224,1024]{2,1,0:T(8,128)} fusion(bf16[16,224,1024]{2,1,0:T(8,128)(2,1)} %bitcast.243, bf16[1024,16,1024]{2,0,1:T(8,128)(2,1)} %all-gather.11.cloned.1.call-done), kind=kOutput, calls=%fused_computation.184 | convolution fusion | flops 7516192768 | bytes 55574528 | tf_op jit(solution)/shard_map/ecd,def->ecf/dot_general | solution.py:216
  298.1 105.8 %all-gather.13.cloned.1.call-done = bf16[512,16,1024]{2,0,1:T(8,128)(2,1)} async-done(((bf16[32,16,1024]{2,0,1:T(8,128)(2,1)}), bf16[512,16,1024]{2,0,1:T(8,128)(2,1)}) %all-gather.13.cloned.1.call-update) | async-done | bytes 16777232 | tf_op jit(solution)/shard_map/all_gather | solution.py:214
  404.0 24.3 %multiply_convert_fusion.2 = (bf16[16,224,512]{2,1,0:T(8,128)(2,1)}, bf16[16,224,512]{2,1,0:T(8,128)(2,1)}, bf16[16,224,512]{2,1,0:T(8,128)(2,1)}) fusion(f32[16,224,1024]{2,1,0:T(8,128)} %fusion.81, bf16[512,16,1024]{2,0,1:T(8,128)(2,1)} %all-gather.13.cloned.1.call-done, f32[16,224,1024]{2,1,0:T(8,128)} %bitcast.241, f32[16,224]{1,0:T(8,128)S(1)} %mul.376), kind=kOutput, calls=%fused_computation.26 | convolution fusion | flops 3792961536 | bytes 57161728 | tf_op jit(solution)/shard_map/ecd,fed->ecf/dot_general | solution.py:221
  428.3 21.6 %fusion.8 = f32[16,224,1024]{2,1,0:T(8,128)} fusion(bf16[1024,16,1024]{2,0,1:T(8,128)(2,1)} %all-gather.11.cloned.1.call-done, bf16[16,224,512]{2,1,0:T(8,128)(2,1)} %get-tuple-element.50, bf16[16,224,512]{2,1,0:T(8,128)(2,1)} %get-tuple-element.49), kind=kOutput, calls=%fused_computation.31 | convolution fusion | flops 7530872832 | bytes 55574528 | tf_op jit(solution)/shard_map/ecf,def->ecd/dot_general | solution.py:231
  449.9 17.1 gather_fusion.4
  473.5 13.5 fusion.82
  487.1 17.0 gather_fusion.1
  526.4 8.6 all-to-all-done.4
  586.3 20.1 %convolution_bitcast_fusion.1 = f32[512,16,1024]{0,2,1:T(8,128)} fusion(bf16[16,224,512]{2,1,0:T(8,128)(2,1)} %get-tuple-element.51, f32[16,224,1024]{2,1,0:T(8,128)} %bitcast.242, f32[16,224]{1,0:T(8,128)S(1)} %mul.376), kind=kOutput, calls=%fused_computation.8 | convolution fusion | flops 3765436416 | bytes 51918848 | tf_op jit(solution)/shard_map/ecf,ecd->fed/dot_general | solution.py:224
  606.4 34.0 %copy.163 = f32[512,16,1024]{2,1,0:T(8,128)} copy(f32[512,16,1024]{0,2,1:T(8,128)} %convolution_bitcast_fusion.1) | data formatting | bytes 67108864 | tf_op jit(solution)/shard_map/ecf,ecd->fed/transpose | solution.py:224
  640.6 29.2 %convolution_bitcast_fusion = f32[1024,16,1024]{0,2,1:T(8,128)} fusion(bf16[16,224,1024]{2,1,0:T(8,128)(2,1)} %bitcast.244, bf16[16,224,512]{2,1,0:T(8,128)(2,1)} %get-tuple-element.50, bf16[16,224,512]{2,1,0:T(8,128)(2,1)} %get-tuple-element.49), kind=kOutput, calls=%fused_computation.6 | convolution fusion | flops 7530872832 | bytes 81788928 | tf_op jit(solution)/shard_map/ecd,ecf->def/dot_general | solution.py:228
  669.7 68.0 %copy.162 = f32[1024,16,1024]{2,1,0:T(8,128)} copy(f32[1024,16,1024]{0,2,1:T(8,128)} %convolution_bitcast_fusion) | data formatting | bytes 134217728 | tf_op jit(solution)/shard_map/ecd,ecf->def/transpose | solution.py:228
  743.9 287.7 %reduce-scatter.14.cloned.1.call-done = f32[32,16,1024]{2,1,0:T(8,128)} async-done(((f32[512,16,1024]{2,1,0:T(8,128)}), f32[32,16,1024]{2,1,0:T(8,128)}) %reduce-scatter.14.cloned.1.call-update) | async-done | bytes 2097168 | tf_op jit(solution)/shard_map/reduce_scatter | solution.py:323
  1034.4 633.0 %reduce-scatter.12.cloned.1.call-done = f32[64,16,1024]{2,1,0:T(8,128)} async-done(((f32[1024,16,1024]{2,1,0:T(8,128)}), f32[64,16,1024]{2,1,0:T(8,128)}) %reduce-scatter.12.cloned.1.call-update) | async-done | bytes 4194320 | tf_op jit(solution)/shard_map/reduce_scatter | solution.py:322
  1673.4 53.5 %reduce-scatter.16.cloned.1.call-done = f32[64,16]{1,0:T(8,128)} async-done(((f32[1024,16]{1,0:T(8,128)}), f32[64,16]{1,0:T(8,128)}) %reduce-scatter.16.cloned.1.call-update) | async-done | bytes 4112
  1732.2 30.1 %all-reduce.6 = (bf16[1024]{0:T(1024)(128)(2,1)S(1)}, bf16[1024]{0:T(1024)(128)(2,1)S(1)}) all-reduce(f32[1024]{0:T(1024)S(1)} %get-tuple-element.34, f32[1024]{0:T(1024)S(1)} %copy-done.48), channel_id=3, replica_groups=mesh['seq'=2,'dp'=16] {'dp'}, use_global_device_ids=true, to_apply=%region_24.25.clone | all-reduce | flops 2048 | bytes 12288
  1772.2 51.8 %all-reduce.12.cloned.1.call-done = (bf16[64,2048]{1,0:T(8,128)(2,1)}, bf16[64,1024]{1,0:T(8,128)(2,1)}, bf16[64,16,1024]{2,1,0:T(8,128)(2,1)}, bf16[32,16,1024]{2,1,0:T(8,128)(2,1)}) async-done(((bf16[64,2048]{1,0:T(8,128)(2,1)}, bf16[64,1024]{1,0:T(8,128)(2,1)}, bf16[64,16,1024]{2,1,0:T(8,128)(2,1)}, bf16[32,16,1024]{2,1,0:T(8,128)(2,1)}), (bf16[64,2048]{1,0:T(8,128)(2,1)}, bf16[64,1024]{1,0:T(8,128)(2,1)}, ...) | async-done | bytes 3538960 | tf_op jit(solution)/shard_map/psum | solution.py:327
  (318 shorter events, 204.9 us)
Async XLA Ops:
  7.2 45.3 %copy-start.59 = (s32[1,256]{1,0:T(1,128)S(1)}, s32[1,256]{1,0:T(1,128)}, u32[]{:S(2)}) copy-start(s32[1,256]{1,0:T(1,128)} %param.12) | copy-start | bytes 3076
  7.2 68.2 %all-gather.7.cloned.1.call-start = ((), (), s32[]{:S(2)}) async-start(), calls=%async_computation.13 | async-start | bytes 4456448 | tf_op jit(solution)/shard_map/all_gather | solution.py:119
  8.0 155.8 %all-gather.9.cloned.1.call-start = ((), (), s32[]{:S(2)}) async-start(), calls=%async_computation.14 | async-start | bytes 2228224 | tf_op jit(solution)/shard_map/all_gather | solution.py:120
  8.7 64.9 %copy-start.10 = (bf16[1,256,1024]{2,1,0:T(8,128)(2,1)S(1)}, bf16[1,256,1024]{2,1,0:T(8,128)(2,1)}, u32[]{:S(2)}) copy-start(bf16[1,256,1024]{2,1,0:T(8,128)(2,1)} %param.11) | copy-start | bytes 1572868
  8.7 266.4 %all-gather.11.cloned.1.call-start = ((), (), s32[]{:S(2)}) async-start(), calls=%async_computation.15 | async-start | bytes 35651584 | tf_op jit(solution)/shard_map/all_gather | solution.py:213
  12.9 391.1 %all-gather.13.cloned.1.call-start = ((), (), s32[]{:S(2)}) async-start(), calls=%async_computation.16 | async-start | bytes 17825792 | tf_op jit(solution)/shard_map/all_gather | solution.py:214
  81.6 19.5 %all-to-all-start = ((bf16[256,2,256]{2,0,1:T(8,128)(2,1)}), bf16[256,2,256]{2,0,1:T(8,128)(2,1)}, u32[]{:S(2)}, u32[]{:S(2)}) async-start(bf16[256,2,256]{2,0,1:T(8,128)(2,1)} %bitcast.262), calls=%async_computation | async-start | bytes 524288 | tf_op jit(solution)/shard_map/all_to_all | solution.py:155
  101.1 9.4 all-to-all-start.1
  110.5 10.3 all-to-all-start.2
  114.3 36.8 %copy-start.8 = (f32[256,1024]{1,0:T(8,128)}, f32[256,1024]{1,0:T(8,128)S(1)}, u32[]{:S(2)}) copy-start(f32[256,1024]{1,0:T(8,128)S(1)} %bitcast_convert_fusion) | copy-start | bytes 3145732
  129.0 34.8 %all-to-all-start.3 = ((bf16[2,256,512]{1,2,0:T(8,128)(2,1)}), bf16[2,256,512]{1,2,0:T(8,128)(2,1)S(1)}, u32[]{:S(2)}, u32[]{:S(2)}) async-start(bf16[2,256,512]{1,2,0:T(8,128)(2,1)} %copy.143), calls=%async_computation.3 | async-start | bytes 1048576 | tf_op jit(solution)/shard_map/all_to_all | solution.py:191
  132.5 607.9 %reduce-scatter.10.cloned.1.call-start = ((), (), s32[]{:S(2)}) async-start(), calls=%async_computation.18 | async-start | bytes 4456448 | tf_op jit(solution)/shard_map/reduce_scatter | solution.py:319
  522.9 12.2 all-to-all-start.4
  550.5 11.1 all-to-all-start.6
  561.6 11.4 all-to-all-start.5
  573.0 8.6 all-to-all-start.7
  576.4 165.6 %reduce-scatter.8.cloned.1.call-start = ((), (), s32[]{:S(2)}) async-start(), calls=%async_computation.17 | async-start | bytes 8912896 | tf_op jit(solution)/shard_map/reduce_scatter | solution.py:318
  586.3 445.4 %reduce-scatter.14.cloned.1.call-start = ((), (), s32[]{:S(2)}) async-start(), calls=%async_computation.20 | async-start | bytes 35651584 | tf_op jit(solution)/shard_map/reduce_scatter | solution.py:323
  640.5 1026.9 %reduce-scatter.12.cloned.1.call-start = ((), (), s32[]{:S(2)}) async-start(), calls=%async_computation.19 | async-start | bytes 71303168 | tf_op jit(solution)/shard_map/reduce_scatter | solution.py:322
  737.7 989.2 %reduce-scatter.16.cloned.1.call-start = ((), (), s32[]{:S(2)}) async-start(), calls=%async_computation.21 | async-start | bytes 557056
  740.3 1083.8 %all-reduce.12.cloned.1.call-start = ((), (), s32[]{:S(2)}) async-start(), calls=%async_computation.22 | async-start | bytes 7077888 | tf_op jit(solution)/shard_map/psum | solution.py:327
  1671.3 61.0 %copy-start.48 = (f32[1024]{0:T(1024)S(1)}, f32[1024]{0:T(1024)}, u32[]{:S(2)}) copy-start(f32[1024]{0:T(1024)} %get-tuple-element.32) | copy-start | bytes 12292
  1671.3 98.6 %copy-start.7 = (f32[256,1024]{1,0:T(8,128)S(1)}, f32[256,1024]{1,0:T(8,128)}, u32[]{:S(2)}) copy-start(f32[256,1024]{1,0:T(8,128)} %copy-done.6) | copy-start | bytes 3145732
  1671.3 98.6 %copy-start.55 = (f32[256]{0:T(256)S(1)}, f32[256]{0:T(256)}, u32[]{:S(2)}) copy-start(f32[256]{0:T(256)} %get-tuple-element.69) | copy-start | bytes 3076
  (56 other events, 545.4 us)
Sparse Core Ops, SparseCore 0:
  10.2 53.3 all-gather.6
  65.8 40.0 all-gather.8
  108.1 167.0 all-gather.10
  277.2 126.7 all-gather.12
  519.8 70.9 reduce-scatter.9
  594.7 102.4 reduce-scatter.7
  701.4 330.1 reduce-scatter.13
  1035.9 631.5 reduce-scatter.11
  1671.6 55.2 reduce-scatter.15
  1730.4 93.6 all-reduce.11
where the time goes:
time: 1850 us; the launch traced here: 1840 us
  waiting for transfers between devices  1240 us (67%)
  local copies, waits for them, and re-layouts  227 us (12%)
  matrix products  172 us (9%)
  blocking collectives  93.7 us (5%)
  other arithmetic  65.2 us (4%)
  starting transfers between devices  29.7 us (2%)
    reduce_scatter x1, waiting for transfers between devices, body(): lax.psum_scatter(gate_up_wgrad, 'dp', scatter_dimension=0, tiled=True)  633 us
    reduce_scatter x1, waiting for transfers between devices, body(): lax.psum_scatter(down_wgrad, 'dp', scatter_dimension=0, tiled=True)  288 us
    all_gather x1, waiting for transfers between devices, body(): lax.all_gather(w_down, 'dp', axis=0, tiled=True)  106 us
    all_gather x1, waiting for transfers between devices, body(): lax.all_gather(w_gate_up, 'dp', axis=0, tiled=True)  75.6 us
    transpose x1, local copies, waits for them, and re-layouts, body(): jnp.einsum('ecd,ecf->def', dispatched, gate_up_grad, preferred_element_ty...  68 us
    unnamed x2, blocking collectives  65.9 us
    unnamed x11, waiting for transfers between devices  55 us
    psum x1, waiting for transfers between devices, body(): lax.psum(shard_qkv.astype(jnp.bfloat16), 'seq').astype(jnp.float32)  51.8 us
  transfers between devices with their start and end apart: 18, of which 11 were waited for; matrix products, arithmetic and copies ran while one was open for 18% of the time, Pallas kernels for 0%

commit v1 on v0

--- a/solution.py
+++ b/solution.py
@@ -15,6 +15,23 @@
 rope_base = 10000.0
 highest = lax.Precision.HIGHEST
 masked_score = -1e30
+
+
+def in_order(blocks, dim):
+    blocks = jnp.moveaxis(blocks, 0, dim)
+    dims = blocks.shape
+    return blocks.reshape(*dims[:dim], dims[dim] * dims[dim + 1], *dims[dim + 2 :])
+
+
+def collect(shard, axis, dim):
+    size = lax.axis_size(axis)
+    ahead = [(i, (i + 1) % size) for i in range(size)]
+    blocks = [shard]
+    while len(blocks) < size:
+        blocks.append(lax.ppermute(blocks[-1], axis, ahead))
+    place = lax.axis_index(axis)
+    blocks = jnp.stack(blocks)[(place - jnp.arange(size)) % size]
+    return in_order(blocks, dim)
 
 
 def rms_normed(token_rows, gain_row):
@@ -211,7 +228,7 @@
     )
     full_gate_up, full_down = (
         lax.all_gather(w_gate_up, "dp", axis=0, tiled=True),
-        lax.all_gather(w_down, "dp", axis=0, tiled=True),
+        collect(w_down, "dp", 0),
     )
     gate_up = jnp.einsum(
         "ecd,def->ecf", dispatched, full_gate_up, preferred_element_type=jnp.float32

time: 1850 us -> 1970 us (1.065)
  local copies, waits for them, and re-layouts: 227 us -> 266 us
  blocking collectives: 93.7 us -> 120 us
  matrix products: 172 us -> 192 us
  waiting for transfers between devices: 1240 us -> 1260 us
    ppermute x0 -> x15, waiting for transfers between devices: none -> 213 us  [collect(): blocks.append(lax.ppermute(blocks[-1], axis, ahead))]
    all_gather x1 -> x0, waiting for transfers between devices: 106 us -> none  [body(): lax.all_gather(w_down, 'dp', axis=0, tiled=True)]
    all_gather x1, waiting for transfers between devices: 75.6 us -> 0.01 us  [body(): lax.all_gather(w_gate_up, 'dp', axis=0, tiled=True)]
    unnamed x136 -> x152, local copies, waits for them, and re-layouts: 14 us -> 45.8 us
    unnamed x2, blocking collectives: 65.9 us -> 91.3 us
    unnamed x11 -> x10, waiting for transfers between devices: 55 us -> 55 us
  transfers between devices with their start and end apart: 18 -> 32, of which waited for: 11 -> 21; matrix products, arithmetic and copies ran while one was open for 18% -> 18% of each run, Pallas kernels for 0% -> 0%
where the time goes in v1:
time: 1970 us; the launch traced here: 1950 us
  waiting for transfers between devices  1260 us (64%)
  local copies, waits for them, and re-layouts  266 us (14%)
  matrix products  192 us (10%)
  blocking collectives  120 us (6%)
  other arithmetic  64.4 us (3%)
  starting transfers between devices  31.6 us (2%)
    reduce_scatter x1, waiting for transfers between devices, body(): lax.psum_scatter(gate_up_wgrad, 'dp', scatter_dimension=0, tiled=True)  633 us
    reduce_scatter x1, waiting for transfers between devices, body(): lax.psum_scatter(down_wgrad, 'dp', scatter_dimension=0, tiled=True)  290 us
    ppermute x15, waiting for transfers between devices, collect(): blocks.append(lax.ppermute(blocks[-1], axis, ahead))  213 us
    unnamed x2, blocking collectives  91.3 us
    transpose x1, local copies, waits for them, and re-layouts, body(): jnp.einsum('ecd,ecf->def', dispatched, gate_up_grad, preferred_element_ty...  68.3 us
    unnamed x10, waiting for transfers between devices  55 us
    psum x1, waiting for transfers between devices, body(): lax.psum(shard_qkv.astype(jnp.bfloat16), 'seq').astype(jnp.float32)  52.1 us
    unnamed x152, local copies, waits for them, and re-layouts  45.8 us
  transfers between devices with their start and end apart: 32, of which 21 were waited for; matrix products, arithmetic and copies ran while one was open for 18% of the time, Pallas kernels for 0%

profile of v1, /device:TPU:0, one launch (start us, length us, event | category | flops | bytes accessed | tf_op | source)
XLA Modules:
  0.0 1953.2 jit_solution(6280340109610934071)
XLA Ops:
  13.4 26.1 %collective-permute-done = bf16[32,16,1024]{2,1,0:T(8,128)(2,1)S(1)} collective-permute-done((bf16[32,16,1024]{2,1,0:T(8,128)(2,1)}, bf16[32,16,1024]{2,1,0:T(8,128)(2,1)S(1)}, u32[]{:S(2)}, u32[]{:S(2)}) %collective-permute-start) | collective-permute-done | bytes 1048608 | tf_op jit(solution)/shard_map/ppermute | solution.py:31
  39.5 33.5 %collective-permute-done.1 = bf16[32,16,1024]{2,1,0:T(8,128)(2,1)S(1)} collective-permute-done((bf16[32,16,1024]{2,1,0:T(8,128)(2,1)S(1)}, bf16[32,16,1024]{2,1,0:T(8,128)(2,1)S(1)}, u32[]{:S(2)}, u32[]{:S(2)}) %collective-permute-start.1) | collective-permute-done | bytes 1048608 | tf_op jit(solution)/shard_map/ppermute | solution.py:31
  93.0 22.2 %collective-permute-done.3 = bf16[32,16,1024]{2,1,0:T(8,128)(2,1)} collective-permute-done((bf16[32,16,1024]{2,1,0:T(8,128)(2,1)}, bf16[32,16,1024]{2,1,0:T(8,128)(2,1)}, u32[]{:S(2)}, u32[]{:S(2)}) %collective-permute-start.3) | collective-permute-done | bytes 1048608 | tf_op jit(solution)/shard_map/ppermute | solution.py:31
  133.3 39.0 %collective-permute-done.5 = bf16[32,16,1024]{2,1,0:T(8,128)(2,1)} collective-permute-done((bf16[32,16,1024]{2,1,0:T(8,128)(2,1)}, bf16[32,16,1024]{2,1,0:T(8,128)(2,1)}, u32[]{:S(2)}, u32[]{:S(2)}) %collective-permute-start.5) | collective-permute-done | bytes 1048608 | tf_op jit(solution)/shard_map/ppermute | solution.py:31
  174.0 61.4 %all-reduce.7 = (bf16[1024]{0:T(1024)(128)(2,1)S(1)}, bf16[1024]{0:T(1024)(128)(2,1)S(1)}) all-reduce(bf16[1024]{0:T(1024)(128)(2,1)S(1)} %dynamic-update-slice, bf16[1024]{0:T(1024)(128)(2,1)S(1)} %dynamic-update-slice.1), channel_id=1, replica_groups=mesh['seq'=2,'dp'=16] {'dp'}, use_global_device_ids=true, to_apply=%add.2 | all-reduce | flops 2048 | bytes 8192
  235.4 18.4 all-gather.1
  282.5 30.2 %collective-permute-done.7 = bf16[32,16,1024]{2,1,0:T(8,128)(2,1)} collective-permute-done((bf16[32,16,1024]{2,1,0:T(8,128)(2,1)}, bf16[32,16,1024]{2,1,0:T(8,128)(2,1)}, u32[]{:S(2)}, u32[]{:S(2)}) %collective-permute-start.7) | collective-permute-done | bytes 1048608 | tf_op jit(solution)/shard_map/ppermute | solution.py:31
  393.3 13.2 collective-permute-done.12
  407.2 18.8 gather_fusion.3
  473.9 21.7 %fusion.86 = f32[16,224,1024]{2,1,0:T(8,128)} fusion(bf16[16,224,1024]{2,1,0:T(8,128)(2,1)} %bitcast.276, bf16[1024,16,1024]{2,0,1:T(8,128)(2,1)} %all-gather.10.cloned.1.call-done), kind=kOutput, calls=%fused_computation.211 | convolution fusion | flops 7516192768 | bytes 55574528 | tf_op jit(solution)/shard_map/ecd,def->ecf/dot_general | solution.py:233
  495.6 27.4 %multiply_convert_fusion.2 = (bf16[16,224,512]{2,1,0:T(8,128)(2,1)}, bf16[16,224,512]{2,1,0:T(8,128)(2,1)}, bf16[16,224,512]{2,1,0:T(8,128)(2,1)}) fusion(f32[16,224,1024]{2,1,0:T(8,128)} %fusion.86, bf16[512,16,1024]{2,1,0:T(8,128)(2,1)} %bitcast.278, f32[16,224,1024]{2,1,0:T(8,128)} %bitcast.274, f32[16,224]{1,0:T(8,128)S(1)} %mul.376), kind=kOutput, calls=%fused_computation.31 | convolution fusion | flops 3792961536 | bytes 57161728 | tf_op jit(solution)/shard_map/ecd,fed->ecf/dot_general | solution.py:238
  523.1 31.7 %fusion.2 = f32[16,224,1024]{2,1,0:T(8,128)} fusion(bf16[16,224,512]{2,1,0:T(8,128)(2,1)} %get-tuple-element.51, bf16[512,16,1024]{2,1,0:T(8,128)(2,1)} %bitcast.279), kind=kOutput, calls=%fused_computation.10 | convolution fusion | flops 3758096384 | bytes 35127296 | tf_op jit(solution)/shard_map/ecf,fed->ecd/dot_general | solution.py:237
  554.8 21.6 %fusion.12 = f32[16,224,1024]{2,1,0:T(8,128)} fusion(bf16[1024,16,1024]{2,0,1:T(8,128)(2,1)} %all-gather.10.cloned.1.call-done, bf16[16,224,512]{2,1,0:T(8,128)(2,1)} %get-tuple-element.50, bf16[16,224,512]{2,1,0:T(8,128)(2,1)} %get-tuple-element.49), kind=kOutput, calls=%fused_computation.36 | convolution fusion | flops 7530872832 | bytes 55574528 | tf_op jit(solution)/shard_map/ecf,def->ecd/dot_general | solution.py:248
  576.4 17.1 gather_fusion.5
  599.9 17.1 gather_fusion.2
  696.0 19.4 convolution_bitcast_fusion.1
  715.4 33.9 %copy.168 = f32[512,16,1024]{2,1,0:T(8,128)} copy(f32[512,16,1024]{0,2,1:T(8,128)} %convolution_bitcast_fusion.1) | data formatting | bytes 67108864 | tf_op jit(solution)/shard_map/ecf,ecd->fed/transpose | solution.py:241
  749.4 28.9 %convolution_bitcast_fusion = f32[1024,16,1024]{0,2,1:T(8,128)} fusion(bf16[16,224,1024]{2,1,0:T(8,128)(2,1)} %bitcast.277, bf16[16,224,512]{2,1,0:T(8,128)(2,1)} %get-tuple-element.50, bf16[16,224,512]{2,1,0:T(8,128)(2,1)} %get-tuple-element.49), kind=kOutput, calls=%fused_computation.7 | convolution fusion | flops 7530872832 | bytes 81788928 | tf_op jit(solution)/shard_map/ecd,ecf->def/dot_general | solution.py:245
  778.3 68.3 %copy.167 = f32[1024,16,1024]{2,1,0:T(8,128)} copy(f32[1024,16,1024]{0,2,1:T(8,128)} %convolution_bitcast_fusion) | data formatting | bytes 134217728 | tf_op jit(solution)/shard_map/ecd,ecf->def/transpose | solution.py:245
  853.2 290.2 %reduce-scatter.14.cloned.1.call-done = f32[32,16,1024]{2,1,0:T(8,128)} async-done(((f32[512,16,1024]{2,1,0:T(8,128)}), f32[32,16,1024]{2,1,0:T(8,128)}) %reduce-scatter.14.cloned.1.call-update) | async-done | bytes 2097168 | tf_op jit(solution)/shard_map/reduce_scatter | solution.py:340
  1146.1 633.0 %reduce-scatter.12.cloned.1.call-done = f32[64,16,1024]{2,1,0:T(8,128)} async-done(((f32[1024,16,1024]{2,1,0:T(8,128)}), f32[64,16,1024]{2,1,0:T(8,128)}) %reduce-scatter.12.cloned.1.call-update) | async-done | bytes 4194320 | tf_op jit(solution)/shard_map/reduce_scatter | solution.py:339
  1785.1 53.5 %reduce-scatter.16.cloned.1.call-done = f32[64,16]{1,0:T(8,128)} async-done(((f32[1024,16]{1,0:T(8,128)}), f32[64,16]{1,0:T(8,128)}) %reduce-scatter.16.cloned.1.call-update) | async-done | bytes 4112
  1843.9 30.0 %all-reduce.6 = (bf16[1024]{0:T(1024)(128)(2,1)S(1)}, bf16[1024]{0:T(1024)(128)(2,1)S(1)}) all-reduce(f32[1024]{0:T(1024)S(1)} %get-tuple-element.34, f32[1024]{0:T(1024)S(1)} %copy-done.50), channel_id=3, replica_groups=mesh['seq'=2,'dp'=16] {'dp'}, use_global_device_ids=true, to_apply=%region_24.25.clone | all-reduce | flops 2048 | bytes 12288
  1883.8 52.1 %all-reduce.12.cloned.1.call-done = (bf16[64,2048]{1,0:T(8,128)(2,1)}, bf16[64,1024]{1,0:T(8,128)(2,1)}, bf16[64,16,1024]{2,1,0:T(8,128)(2,1)}, bf16[32,16,1024]{2,1,0:T(8,128)(2,1)}) async-done(((bf16[64,2048]{1,0:T(8,128)(2,1)}, bf16[64,1024]{1,0:T(8,128)(2,1)}, bf16[64,16,1024]{2,1,0:T(8,128)(2,1)}, bf16[32,16,1024]{2,1,0:T(8,128)(2,1)}), (bf16[64,2048]{1,0:T(8,128)(2,1)}, bf16[64,1024]{1,0:T(8,128)(2,1)}, ...) | async-done | bytes 3538960 | tf_op jit(solution)/shard_map/psum | solution.py:344
  (366 shorter events, 327.6 us)
Async XLA Ops:
  7.2 307.7 %all-gather.6.cloned.1.call-start = ((), (), s32[]{:S(2)}) async-start(), calls=%async_computation.13 | async-start | bytes 4456448 | tf_op jit(solution)/shard_map/all_gather | solution.py:136
  8.0 381.3 %all-gather.8.cloned.1.call-start = ((), (), s32[]{:S(2)}) async-start(), calls=%async_computation.14 | async-start | bytes 2228224 | tf_op jit(solution)/shard_map/all_gather | solution.py:137
  8.7 465.2 %all-gather.10.cloned.1.call-start = ((), (), s32[]{:S(2)}) async-start(), calls=%async_computation.15 | async-start | bytes 35651584 | tf_op jit(solution)/shard_map/all_gather | solution.py:230
  12.9 26.6 %collective-permute-start = (bf16[32,16,1024]{2,1,0:T(8,128)(2,1)}, bf16[32,16,1024]{2,1,0:T(8,128)(2,1)S(1)}, u32[]{:S(2)}, u32[]{:S(2)}) collective-permute-start(bf16[32,16,1024]{2,1,0:T(8,128)(2,1)} %param.20), channel_id=1, source_target_pairs={{0,1},{1,2},{2,3},{3,4},{4,5},{5,6},{6,7},{7,8},{8,9},{9,10},{10,1... | collective-permute-start | bytes 3145736 | tf_op jit(solution)/shard_map/ppermute | solution.py:31
  39.5 33.5 %collective-permute-start.1 = (bf16[32,16,1024]{2,1,0:T(8,128)(2,1)S(1)}, bf16[32,16,1024]{2,1,0:T(8,128)(2,1)S(1)}, u32[]{:S(2)}, u32[]{:S(2)}) collective-permute-start(bf16[32,16,1024]{2,1,0:T(8,128)(2,1)S(1)} %collective-permute-done), channel_id=1, source_target_pairs={{0,1},{1,2},{2,3},{3,4},{4,5},{5,6},{6,7},{7,8},{8,9},{9,10},{10,1... | collective-permute-start | bytes 3145736 | tf_op jit(solution)/shard_map/ppermute | solution.py:31
  73.0 19.6 %collective-permute-start.2 = (bf16[32,16,1024]{2,1,0:T(8,128)(2,1)S(1)}, bf16[32,16,1024]{2,1,0:T(8,128)(2,1)}, u32[]{:S(2)}, u32[]{:S(2)}) collective-permute-start(bf16[32,16,1024]{2,1,0:T(8,128)(2,1)S(1)} %collective-permute-done.1), channel_id=1, source_target_pairs={{0,1},{1,2},{2,3},{3,4},{4,5},{5,6},{6,7},{7,8},{8,9},{9,10},{10,1... | collective-permute-start | bytes 3145736 | tf_op jit(solution)/shard_map/ppermute | solution.py:31
  92.6 22.5 %collective-permute-start.3 = (bf16[32,16,1024]{2,1,0:T(8,128)(2,1)}, bf16[32,16,1024]{2,1,0:T(8,128)(2,1)}, u32[]{:S(2)}, u32[]{:S(2)}) collective-permute-start(bf16[32,16,1024]{2,1,0:T(8,128)(2,1)} %collective-permute-done.2), channel_id=1, source_target_pairs={{0,1},{1,2},{2,3},{3,4},{4,5},{5,6},{6,7},{7,8},{8,9},{9,10},{10,1... | collective-permute-start | bytes 3145736 | tf_op jit(solution)/shard_map/ppermute | solution.py:31
  115.1 17.3 collective-permute-start.4
  132.4 39.8 %collective-permute-start.5 = (bf16[32,16,1024]{2,1,0:T(8,128)(2,1)}, bf16[32,16,1024]{2,1,0:T(8,128)(2,1)}, u32[]{:S(2)}, u32[]{:S(2)}) collective-permute-start(bf16[32,16,1024]{2,1,0:T(8,128)(2,1)} %collective-permute-done.4), channel_id=1, source_target_pairs={{0,1},{1,2},{2,3},{3,4},{4,5},{5,6},{6,7},{7,8},{8,9},{9,10},{10,1... | collective-permute-start | bytes 3145736 | tf_op jit(solution)/shard_map/ppermute | solution.py:31
  172.3 100.5 %collective-permute-start.6 = (bf16[32,16,1024]{2,1,0:T(8,128)(2,1)}, bf16[32,16,1024]{2,1,0:T(8,128)(2,1)}, u32[]{:S(2)}, u32[]{:S(2)}) collective-permute-start(bf16[32,16,1024]{2,1,0:T(8,128)(2,1)} %collective-permute-done.5), channel_id=1, source_target_pairs={{0,1},{1,2},{2,3},{3,4},{4,5},{5,6},{6,7},{7,8},{8,9},{9,10},{10,1... | collective-permute-start | bytes 3145736 | tf_op jit(solution)/shard_map/ppermute | solution.py:31
  272.8 39.8 %collective-permute-start.7 = (bf16[32,16,1024]{2,1,0:T(8,128)(2,1)}, bf16[32,16,1024]{2,1,0:T(8,128)(2,1)}, u32[]{:S(2)}, u32[]{:S(2)}) collective-permute-start(bf16[32,16,1024]{2,1,0:T(8,128)(2,1)} %collective-permute-done.6), channel_id=1, source_target_pairs={{0,1},{1,2},{2,3},{3,4},{4,5},{5,6},{6,7},{7,8},{8,9},{9,10},{10,1... | collective-permute-start | bytes 3145736 | tf_op jit(solution)/shard_map/ppermute | solution.py:31
  312.6 25.0 %collective-permute-start.8 = (bf16[32,16,1024]{2,1,0:T(8,128)(2,1)}, bf16[32,16,1024]{2,1,0:T(8,128)(2,1)}, u32[]{:S(2)}, u32[]{:S(2)}) collective-permute-start(bf16[32,16,1024]{2,1,0:T(8,128)(2,1)} %collective-permute-done.7), channel_id=1, source_target_pairs={{0,1},{1,2},{2,3},{3,4},{4,5},{5,6},{6,7},{7,8},{8,9},{9,10},{10,1... | collective-permute-start | bytes 3145736 | tf_op jit(solution)/shard_map/ppermute | solution.py:31
  320.5 24.4 %all-to-all-start = ((bf16[256,2,256]{2,0,1:T(8,128)(2,1)}), bf16[256,2,256]{2,0,1:T(8,128)(2,1)}, u32[]{:S(2)}, u32[]{:S(2)}) async-start(bf16[256,2,256]{2,0,1:T(8,128)(2,1)} %bitcast.266), calls=%async_computation | async-start | bytes 524288 | tf_op jit(solution)/shard_map/all_to_all | solution.py:172
  337.6 17.2 collective-permute-start.9
  354.8 17.2 collective-permute-start.10
  372.1 17.2 collective-permute-start.11
  378.2 471.4 %reduce-scatter.10.cloned.1.call-start = ((), (), s32[]{:S(2)}) async-start(), calls=%async_computation.17 | async-start | bytes 4456448 | tf_op jit(solution)/shard_map/reduce_scatter | solution.py:336
  389.3 17.2 collective-permute-start.12
  406.5 36.2 %collective-permute-start.13 = (bf16[32,16,1024]{2,1,0:T(8,128)(2,1)}, bf16[32,16,1024]{2,1,0:T(8,128)(2,1)S(1)}, u32[]{:S(2)}, u32[]{:S(2)}) collective-permute-start(bf16[32,16,1024]{2,1,0:T(8,128)(2,1)} %collective-permute-done.12), channel_id=1, source_target_pairs={{0,1},{1,2},{2,3},{3,4},{4,5},{5,6},{6,7},{7,8},{8,9},{9,10},{10,1... | collective-permute-start | bytes 3145736 | tf_op jit(solution)/shard_map/ppermute | solution.py:31
  686.1 165.2 %reduce-scatter.8.cloned.1.call-start = ((), (), s32[]{:S(2)}) async-start(), calls=%async_computation.16 | async-start | bytes 8912896 | tf_op jit(solution)/shard_map/reduce_scatter | solution.py:335
  696.0 447.4 %reduce-scatter.14.cloned.1.call-start = ((), (), s32[]{:S(2)}) async-start(), calls=%async_computation.19 | async-start | bytes 35651584 | tf_op jit(solution)/shard_map/reduce_scatter | solution.py:340
  749.4 1029.7 %reduce-scatter.12.cloned.1.call-start = ((), (), s32[]{:S(2)}) async-start(), calls=%async_computation.18 | async-start | bytes 71303168 | tf_op jit(solution)/shard_map/reduce_scatter | solution.py:339
  846.7 991.9 %reduce-scatter.16.cloned.1.call-start = ((), (), s32[]{:S(2)}) async-start(), calls=%async_computation.20 | async-start | bytes 557056
  849.3 1086.6 %all-reduce.12.cloned.1.call-start = ((), (), s32[]{:S(2)}) async-start(), calls=%async_computation.21 | async-start | bytes 7077888 | tf_op jit(solution)/shard_map/psum | solution.py:344
  (72 other events, 2961.3 us)
Sparse Core Ops, SparseCore 0:
  10.2 61.4 all-gather.5
  73.9 47.2 all-gather.7
  123.4 205.9 all-gather.9
  632.6 70.0 reduce-scatter.9
  706.6 102.4 reduce-scatter.7
  813.2 330.1 reduce-scatter.13
  1147.6 631.4 reduce-scatter.11
  1783.2 55.2 reduce-scatter.15
  1842.2 93.6 all-reduce.11
